TPU v7x, 32 devices: a whole 2x2x4 slice. The times are simulated.
32 devices in a mesh: grp: 1, ev: 32 (over z, y, x, core).
Axes of the slice: x: 2, y: 2, z: 4, core: 2. Of those that a mesh axis runs over, the one named last changes fastest.
Arguments:
- windows: bfloat16 [256, 3, 64, 1024], P(('grp', 'ev')), may hold values from -400 to 400, as said below
- rotation: bfloat16 [256, 3, 64], P(('grp', 'ev')), may hold values from -3 to 3
- source_inverse: bfloat16 [256, 1024], P(('grp', 'ev')), may hold values from -3.4 to 3.4
- send_rows: int32 [1024, 64], P(('grp', 'ev')), may hold values from 0 to 511, as said below
- tile_station: int32 [2048], P(('grp', 'ev')), may hold values from 0 to 63, as said below
- tile_count: int32 [2048], P(('grp', 'ev')), may hold values from 16 to 128
- pair_rows: int32 [2, 262144], P(None, ('grp', 'ev')), may hold values from 0 to 2047, as said below
Outputs:
- correlation: float32 [262144, 255], P(('grp', 'ev'))
Inputs may be any that keep to these rules, and one draw needn't show every extreme that they name: Each event's windows carry a scale of their own, and each station's another. `send_rows`: row j of the block of device o names the rows of device o sent to device j, each as local event times 64 plus station, with the station of the tile whose residue matches the receiving slot (o * 64 + k) mod 64. `tile_station`: tile t of a device is fed by received slots r with r mod 64 = t mod 64, all at the tile's station. `pair_rows`: entries count the rows a device receives by sending device then slot; both members of a slot lie at its tile's station.
All inputs are finite; a program needn't handle non-finite values.
Results may differ from a plain program's by a relative error of at most 0.007.
Values may be sent and summed in bfloat16 or wider, within the bound.
No kernel may reach another device: no remote copies, remote signals or barrier semaphores. Data moves between devices by JAX's collectives and lax.ppermute only.
A program may use at most 64 MiB of HBM per device.

v0:
```python
from functools import partial
import math
import jax
import jax.numpy as jnp
from jax import lax
from jax.sharding import PartitionSpec as P

LAGS = 255
epsilon = 1e-06


def spectral_table(length):
    half_len = length // 2
    samples = jnp.arange(length, dtype=jnp.int32)[:, None]
    frequency = jnp.arange(half_len, dtype=jnp.int32)[None, :]
    angles = (samples * frequency % length).astype(jnp.float32) * (2.0 * math.pi / length)
    factor = 1.0 / math.sqrt(length)
    return jnp.concatenate([jnp.cos(angles) * factor, -jnp.sin(angles) * factor], axis=1).astype(
        jnp.bfloat16
    )


def lag_table(length, lag_count):
    half_len = length // 2
    frequency = jnp.arange(half_len, dtype=jnp.int32)[:, None]
    shifts = jnp.arange(lag_count, dtype=jnp.int32)[None, :] - lag_count // 2
    angles = (frequency * shifts % length).astype(jnp.float32) * (2.0 * math.pi / length)
    factor = 1.0 / math.sqrt(half_len)
    return jnp.concatenate([jnp.cos(angles) * factor, -jnp.sin(angles) * factor], axis=0).astype(
        jnp.bfloat16
    )


def event_spectra(windows, rotation, source_inverse, dft_table):
    half_len = dft_table.shape[1] // 2
    transverse = jnp.sum(
        rotation.astype(jnp.float32)[..., None] * windows.astype(jnp.float32), axis=1
    ).astype(jnp.bfloat16)
    events, stations, length = transverse.shape
    spectrum = jnp.dot(
        transverse.reshape(events * stations, length), dft_table, preferred_element_type=jnp.float32
    )
    spectrum = spectrum.reshape(events, stations, length)
    filter_gain = source_inverse.astype(jnp.float32)[:, None, :]
    real_in, imag_in = (spectrum[..., :half_len], spectrum[..., half_len:])
    real_gain, imag_gain = (filter_gain[..., :half_len], filter_gain[..., half_len:])
    return jnp.concatenate(
        [real_in * real_gain - imag_in * imag_gain, real_in * imag_gain + imag_in * real_gain],
        axis=-1,
    )


def correlate_group(spectra, lag_tab, tile_pairs, pieces):
    first_rows, second_rows, weights, counts = pieces
    half_len = spectra.shape[1] // 2
    first_spec = spectra[first_rows].astype(jnp.float32)
    second_spec = spectra[second_rows].astype(jnp.float32)
    first_re, first_im = (first_spec[:, :half_len], first_spec[:, half_len:])
    second_re, second_im = (second_spec[:, :half_len], second_spec[:, half_len:])
    row_weight = jnp.repeat(weights, tile_pairs, axis=0)
    cross_spec = jnp.concatenate(
        [
            (first_re * second_re + first_im * second_im) * row_weight,
            (first_im * second_re - first_re * second_im) * row_weight,
        ],
        axis=1,
    ).astype(jnp.bfloat16)
    lagged = jnp.dot(cross_spec, lag_tab, preferred_element_type=jnp.float32)
    live_rows = jnp.arange(lagged.shape[0], dtype=jnp.int32) % tile_pairs < jnp.repeat(
        counts, tile_pairs
    )
    return jnp.where(live_rows[:, None], lagged, jnp.zeros_like(lagged))


def shards(windows, rotation, source_inverse, send_rows, tile_station, tile_count, pair_rows):
    ev_dev, components, stations, length = windows.shape
    half_len = length // 2
    owners = lax.axis_size("ev")
    dft_table = spectral_table(length)
    deconvolved = event_spectra(windows, rotation, source_inverse, dft_table)
    local_power = jnp.sum(
        deconvolved[..., :half_len] ** 2 + deconvolved[..., half_len:] ** 2, axis=0
    )
    power_sum = lax.psum(local_power, "ev")
    weight = 1.0 / (power_sum / (ev_dev * owners) + epsilon)
    capacity = send_rows.shape[1]
    slot_total = owners * capacity
    own_rows = deconvolved.astype(jnp.bfloat16).reshape(ev_dev * stations, length)
    received = lax.all_to_all(own_rows[send_rows], "ev", split_axis=0, concat_axis=0, tiled=True)
    received = received.reshape(slot_total, length)
    tiles_dev = tile_station.shape[0]
    tile_pairs = pair_rows.shape[1] // tiles_dev
    onehot = (tile_station[:, None] == jnp.arange(stations, dtype=jnp.int32)[None, :]).astype(
        jnp.float32
    )
    tile_weight = jnp.dot(onehot, weight, precision=lax.Precision.HIGHEST)
    groups = tiles_dev // 4
    group_rows = 4 * tile_pairs
    correlate = partial(correlate_group, received, lag_table(length, LAGS), tile_pairs)
    result = lax.map(
        correlate,
        (
            pair_rows[0].reshape(groups, group_rows),
            pair_rows[1].reshape(groups, group_rows),
            tile_weight.reshape(groups, 4, half_len),
            tile_count.reshape(groups, 4),
        ),
    )
    return result.reshape(groups * group_rows, LAGS)


def solution(mesh):
    in_specs = (
        P(("grp", "ev"), None, None, None),
        P(("grp", "ev"), None, None),
        P(("grp", "ev"), None),
        P(("grp", "ev"), None),
        P(("grp", "ev")),
        P(("grp", "ev")),
        P(None, ("grp", "ev")),
    )
    out_specs = P(("grp", "ev"), None)
    return jax.shard_map(shards, mesh=mesh, in_specs=in_specs, out_specs=out_specs, check_vma=False)
```

profile of v0, /device:TPU:0, one launch (start us, length us, event | category | flops | bytes accessed | tf_op | source)
XLA Modules:
  0.0 418.1 jit_solution(10348635386327450920)
XLA Ops:
  6.5 8.6 %multiply_convert_fusion = (bf16[1024,512]{1,0:T(8,128)(2,1)S(1)}, bf16[1024,512]{1,0:T(8,128)(2,1)S(1)}) fusion(), kind=kLoop, calls=%fused_computation.38 | loop fusion | flops 9961472 | bytes 2097152 | tf_op jit(solution)/shard_map/convert.10
  15.3 2.7 multiply_reduce_fusion
  18.0 1.2 fusion.16
  19.3 1.1 add_reduce_fusion
  20.5 9.7 %gather_fusion.2 = bf16[2048,1024]{1,0:T(8,128)(2,1)} fusion(bf16[512,1024]{1,0:T(8,128)(2,1)S(1)} %pad_maximum_fusion, s32[2048]{0:T(1024)S(1)} %broadcast_clamp_fusion), kind=kCustom, calls=%fused_computation.2 | custom fusion | bytes 8396800 | tf_op jit(solution)/shard_map/gather | solution.py:89
  30.1 7.5 %all-to-all-start = ((bf16[32,64,1024]{2,1,0:T(8,128)(2,1)}), bf16[32,64,1024]{2,1,0:T(8,128)(2,1)}, u32[]{:S(2)}, u32[]{:S(2)}) async-start(bf16[32,64,1024]{2,1,0:T(8,128)(2,1)} %bitcast.58), calls=%async_computation | async-start | bytes 8388608 | tf_op jit(solution)/shard_map/all_to_all | solution.py:89
  37.6 0.7 all-reduce.2.cloned.1.call-update
  38.6 2.3 multiply_convert_fusion.3
  40.9 0.9 pad_maximum_fusion.1
  41.8 148.0 %all-reduce.2.cloned.1.call-done = f32[64,512]{1,0:T(8,128)} async-done(((f32[64,512]{1,0:T(8,128)}), f32[64,512]{1,0:T(8,128)}) %all-reduce.2.cloned.1.call-update) | async-done | bytes 131088 | tf_op jit(solution)/shard_map/psum | solution.py:84
  189.8 1.1 fusion.31
  191.1 220.2 %while.12 = (s32[]{:T(128)}, f32[16,512,255]{2,1,0:T(8,128)}, s32[16,4]{1,0:T(8,128)S(1)}, s32[16,512]{1,0:T(8,128)S(1)}, bf16[2048,1024]{1,0:T(8,128)(2,1)}, /*...) while((s32[]{:T(128)}, f32[16,512,255]{2,1,0:T(8,128)}, ...), condition=%wide.region_4.5_spmd, body=%wide.region_3.4_spmd.sunk | while | flops 273293312 | bytes 19963572 | solution.py:100
  191.1 5.5 %gather_fusion = bf16[512,1024]{1,0:T(8,128)(2,1)S(1)} fusion(bf16[2048,1024]{1,0:T(8,128)(2,1)} %get-tuple-element.218, s32[1024]{0:T(1024)S(1)} %pad_clamp_fusion.4), kind=kCustom, calls=%fused_computation.1.clone.1 | custom fusion | bytes 2099200 | tf_op jit(solution)/shard_map/while/body/eval_jaxpr/gather | solution.py:57
  196.8 5.5 %gather_fusion.1 = bf16[512,1024]{1,0:T(8,128)(2,1)S(1)} fusion(bf16[2048,1024]{1,0:T(8,128)(2,1)} %get-tuple-element.218, s32[1024]{0:T(1024)S(1)} %pad_clamp_fusion.5), kind=kCustom, calls=%fused_computation.clone.1 | custom fusion | bytes 2099200 | tf_op jit(solution)/shard_map/while/body/eval_jaxpr/gather | solution.py:56
  203.6 1.2 fusion.56
  204.9 5.5 %gather_fusion = bf16[512,1024]{1,0:T(8,128)(2,1)S(1)} fusion(bf16[2048,1024]{1,0:T(8,128)(2,1)} %get-tuple-element.218, s32[1024]{0:T(1024)S(1)} %pad_clamp_fusion.4), kind=kCustom, calls=%fused_computation.1.clone.1 | custom fusion | bytes 2099200 | tf_op jit(solution)/shard_map/while/body/eval_jaxpr/gather | solution.py:57
  210.6 5.5 %gather_fusion.1 = bf16[512,1024]{1,0:T(8,128)(2,1)S(1)} fusion(bf16[2048,1024]{1,0:T(8,128)(2,1)} %get-tuple-element.218, s32[1024]{0:T(1024)S(1)} %pad_clamp_fusion.5), kind=kCustom, calls=%fused_computation.clone.1 | custom fusion | bytes 2099200 | tf_op jit(solution)/shard_map/while/body/eval_jaxpr/gather | solution.py:56
  216.3 0.6 fusion.53
  217.4 1.2 fusion.56
  218.6 5.5 %gather_fusion = bf16[512,1024]{1,0:T(8,128)(2,1)S(1)} fusion(bf16[2048,1024]{1,0:T(8,128)(2,1)} %get-tuple-element.218, s32[1024]{0:T(1024)S(1)} %pad_clamp_fusion.4), kind=kCustom, calls=%fused_computation.1.clone.1 | custom fusion | bytes 2099200 | tf_op jit(solution)/shard_map/while/body/eval_jaxpr/gather | solution.py:57
  224.4 5.5 %gather_fusion.1 = bf16[512,1024]{1,0:T(8,128)(2,1)S(1)} fusion(bf16[2048,1024]{1,0:T(8,128)(2,1)} %get-tuple-element.218, s32[1024]{0:T(1024)S(1)} %pad_clamp_fusion.5), kind=kCustom, calls=%fused_computation.clone.1 | custom fusion | bytes 2099200 | tf_op jit(solution)/shard_map/while/body/eval_jaxpr/gather | solution.py:56
  230.1 0.6 fusion.53
  231.1 1.2 fusion.56
  232.4 5.5 %gather_fusion = bf16[512,1024]{1,0:T(8,128)(2,1)S(1)} fusion(bf16[2048,1024]{1,0:T(8,128)(2,1)} %get-tuple-element.218, s32[1024]{0:T(1024)S(1)} %pad_clamp_fusion.4), kind=kCustom, calls=%fused_computation.1.clone.1 | custom fusion | bytes 2099200 | tf_op jit(solution)/shard_map/while/body/eval_jaxpr/gather | solution.py:57
  238.1 5.5 %gather_fusion.1 = bf16[512,1024]{1,0:T(8,128)(2,1)S(1)} fusion(bf16[2048,1024]{1,0:T(8,128)(2,1)} %get-tuple-element.218, s32[1024]{0:T(1024)S(1)} %pad_clamp_fusion.5), kind=kCustom, calls=%fused_computation.clone.1 | custom fusion | bytes 2099200 | tf_op jit(solution)/shard_map/while/body/eval_jaxpr/gather | solution.py:56
  243.9 0.6 fusion.53
  244.9 1.2 fusion.56
  246.2 5.5 %gather_fusion = bf16[512,1024]{1,0:T(8,128)(2,1)S(1)} fusion(bf16[2048,1024]{1,0:T(8,128)(2,1)} %get-tuple-element.218, s32[1024]{0:T(1024)S(1)} %pad_clamp_fusion.4), kind=kCustom, calls=%fused_computation.1.clone.1 | custom fusion | bytes 2099200 | tf_op jit(solution)/shard_map/while/body/eval_jaxpr/gather | solution.py:57
  251.9 5.5 %gather_fusion.1 = bf16[512,1024]{1,0:T(8,128)(2,1)S(1)} fusion(bf16[2048,1024]{1,0:T(8,128)(2,1)} %get-tuple-element.218, s32[1024]{0:T(1024)S(1)} %pad_clamp_fusion.5), kind=kCustom, calls=%fused_computation.clone.1 | custom fusion | bytes 2099200 | tf_op jit(solution)/shard_map/while/body/eval_jaxpr/gather | solution.py:56
  258.7 1.2 fusion.56
  259.9 5.5 %gather_fusion = bf16[512,1024]{1,0:T(8,128)(2,1)S(1)} fusion(bf16[2048,1024]{1,0:T(8,128)(2,1)} %get-tuple-element.218, s32[1024]{0:T(1024)S(1)} %pad_clamp_fusion.4), kind=kCustom, calls=%fused_computation.1.clone.1 | custom fusion | bytes 2099200 | tf_op jit(solution)/shard_map/while/body/eval_jaxpr/gather | solution.py:57
  265.6 5.5 %gather_fusion.1 = bf16[512,1024]{1,0:T(8,128)(2,1)S(1)} fusion(bf16[2048,1024]{1,0:T(8,128)(2,1)} %get-tuple-element.218, s32[1024]{0:T(1024)S(1)} %pad_clamp_fusion.5), kind=kCustom, calls=%fused_computation.clone.1 | custom fusion | bytes 2099200 | tf_op jit(solution)/shard_map/while/body/eval_jaxpr/gather | solution.py:56
  271.4 0.6 fusion.53
  272.4 1.2 fusion.56
  273.7 5.5 %gather_fusion = bf16[512,1024]{1,0:T(8,128)(2,1)S(1)} fusion(bf16[2048,1024]{1,0:T(8,128)(2,1)} %get-tuple-element.218, s32[1024]{0:T(1024)S(1)} %pad_clamp_fusion.4), kind=kCustom, calls=%fused_computation.1.clone.1 | custom fusion | bytes 2099200 | tf_op jit(solution)/shard_map/while/body/eval_jaxpr/gather | solution.py:57
  279.4 5.5 %gather_fusion.1 = bf16[512,1024]{1,0:T(8,128)(2,1)S(1)} fusion(bf16[2048,1024]{1,0:T(8,128)(2,1)} %get-tuple-element.218, s32[1024]{0:T(1024)S(1)} %pad_clamp_fusion.5), kind=kCustom, calls=%fused_computation.clone.1 | custom fusion | bytes 2099200 | tf_op jit(solution)/shard_map/while/body/eval_jaxpr/gather | solution.py:56
  286.2 1.2 fusion.56
  287.4 5.5 %gather_fusion = bf16[512,1024]{1,0:T(8,128)(2,1)S(1)} fusion(bf16[2048,1024]{1,0:T(8,128)(2,1)} %get-tuple-element.218, s32[1024]{0:T(1024)S(1)} %pad_clamp_fusion.4), kind=kCustom, calls=%fused_computation.1.clone.1 | custom fusion | bytes 2099200 | tf_op jit(solution)/shard_map/while/body/eval_jaxpr/gather | solution.py:57
  293.2 5.5 %gather_fusion.1 = bf16[512,1024]{1,0:T(8,128)(2,1)S(1)} fusion(bf16[2048,1024]{1,0:T(8,128)(2,1)} %get-tuple-element.218, s32[1024]{0:T(1024)S(1)} %pad_clamp_fusion.5), kind=kCustom, calls=%fused_computation.clone.1 | custom fusion | bytes 2099200 | tf_op jit(solution)/shard_map/while/body/eval_jaxpr/gather | solution.py:56
  299.9 1.2 fusion.56
  301.2 5.5 %gather_fusion = bf16[512,1024]{1,0:T(8,128)(2,1)S(1)} fusion(bf16[2048,1024]{1,0:T(8,128)(2,1)} %get-tuple-element.218, s32[1024]{0:T(1024)S(1)} %pad_clamp_fusion.4), kind=kCustom, calls=%fused_computation.1.clone.1 | custom fusion | bytes 2099200 | tf_op jit(solution)/shard_map/while/body/eval_jaxpr/gather | solution.py:57
  306.9 5.5 %gather_fusion.1 = bf16[512,1024]{1,0:T(8,128)(2,1)S(1)} fusion(bf16[2048,1024]{1,0:T(8,128)(2,1)} %get-tuple-element.218, s32[1024]{0:T(1024)S(1)} %pad_clamp_fusion.5), kind=kCustom, calls=%fused_computation.clone.1 | custom fusion | bytes 2099200 | tf_op jit(solution)/shard_map/while/body/eval_jaxpr/gather | solution.py:56
  313.7 1.2 fusion.56
  315.0 5.5 %gather_fusion = bf16[512,1024]{1,0:T(8,128)(2,1)S(1)} fusion(bf16[2048,1024]{1,0:T(8,128)(2,1)} %get-tuple-element.218, s32[1024]{0:T(1024)S(1)} %pad_clamp_fusion.4), kind=kCustom, calls=%fused_computation.1.clone.1 | custom fusion | bytes 2099200 | tf_op jit(solution)/shard_map/while/body/eval_jaxpr/gather | solution.py:57
  320.7 5.5 %gather_fusion.1 = bf16[512,1024]{1,0:T(8,128)(2,1)S(1)} fusion(bf16[2048,1024]{1,0:T(8,128)(2,1)} %get-tuple-element.218, s32[1024]{0:T(1024)S(1)} %pad_clamp_fusion.5), kind=kCustom, calls=%fused_computation.clone.1 | custom fusion | bytes 2099200 | tf_op jit(solution)/shard_map/while/body/eval_jaxpr/gather | solution.py:56
  327.5 1.2 fusion.56
  328.7 5.5 %gather_fusion = bf16[512,1024]{1,0:T(8,128)(2,1)S(1)} fusion(bf16[2048,1024]{1,0:T(8,128)(2,1)} %get-tuple-element.218, s32[1024]{0:T(1024)S(1)} %pad_clamp_fusion.4), kind=kCustom, calls=%fused_computation.1.clone.1 | custom fusion | bytes 2099200 | tf_op jit(solution)/shard_map/while/body/eval_jaxpr/gather | solution.py:57
  334.4 5.5 %gather_fusion.1 = bf16[512,1024]{1,0:T(8,128)(2,1)S(1)} fusion(bf16[2048,1024]{1,0:T(8,128)(2,1)} %get-tuple-element.218, s32[1024]{0:T(1024)S(1)} %pad_clamp_fusion.5), kind=kCustom, calls=%fused_computation.clone.1 | custom fusion | bytes 2099200 | tf_op jit(solution)/shard_map/while/body/eval_jaxpr/gather | solution.py:56
  341.2 1.2 fusion.56
  342.5 5.5 %gather_fusion = bf16[512,1024]{1,0:T(8,128)(2,1)S(1)} fusion(bf16[2048,1024]{1,0:T(8,128)(2,1)} %get-tuple-element.218, s32[1024]{0:T(1024)S(1)} %pad_clamp_fusion.4), kind=kCustom, calls=%fused_computation.1.clone.1 | custom fusion | bytes 2099200 | tf_op jit(solution)/shard_map/while/body/eval_jaxpr/gather | solution.py:57
  348.2 5.5 %gather_fusion.1 = bf16[512,1024]{1,0:T(8,128)(2,1)S(1)} fusion(bf16[2048,1024]{1,0:T(8,128)(2,1)} %get-tuple-element.218, s32[1024]{0:T(1024)S(1)} %pad_clamp_fusion.5), kind=kCustom, calls=%fused_computation.clone.1 | custom fusion | bytes 2099200 | tf_op jit(solution)/shard_map/while/body/eval_jaxpr/gather | solution.py:56
  355.0 1.2 fusion.56
  356.2 5.5 %gather_fusion = bf16[512,1024]{1,0:T(8,128)(2,1)S(1)} fusion(bf16[2048,1024]{1,0:T(8,128)(2,1)} %get-tuple-element.218, s32[1024]{0:T(1024)S(1)} %pad_clamp_fusion.4), kind=kCustom, calls=%fused_computation.1.clone.1 | custom fusion | bytes 2099200 | tf_op jit(solution)/shard_map/while/body/eval_jaxpr/gather | solution.py:57
  362.0 5.5 %gather_fusion.1 = bf16[512,1024]{1,0:T(8,128)(2,1)S(1)} fusion(bf16[2048,1024]{1,0:T(8,128)(2,1)} %get-tuple-element.218, s32[1024]{0:T(1024)S(1)} %pad_clamp_fusion.5), kind=kCustom, calls=%fused_computation.clone.1 | custom fusion | bytes 2099200 | tf_op jit(solution)/shard_map/while/body/eval_jaxpr/gather | solution.py:56
  368.7 1.2 fusion.56
  370.0 5.5 %gather_fusion = bf16[512,1024]{1,0:T(8,128)(2,1)S(1)} fusion(bf16[2048,1024]{1,0:T(8,128)(2,1)} %get-tuple-element.218, s32[1024]{0:T(1024)S(1)} %pad_clamp_fusion.4), kind=kCustom, calls=%fused_computation.1.clone.1 | custom fusion | bytes 2099200 | tf_op jit(solution)/shard_map/while/body/eval_jaxpr/gather | solution.py:57
  375.7 5.5 %gather_fusion.1 = bf16[512,1024]{1,0:T(8,128)(2,1)S(1)} fusion(bf16[2048,1024]{1,0:T(8,128)(2,1)} %get-tuple-element.218, s32[1024]{0:T(1024)S(1)} %pad_clamp_fusion.5), kind=kCustom, calls=%fused_computation.clone.1 | custom fusion | bytes 2099200 | tf_op jit(solution)/shard_map/while/body/eval_jaxpr/gather | solution.py:56
  382.5 1.2 fusion.56
  383.8 5.5 %gather_fusion = bf16[512,1024]{1,0:T(8,128)(2,1)S(1)} fusion(bf16[2048,1024]{1,0:T(8,128)(2,1)} %get-tuple-element.218, s32[1024]{0:T(1024)S(1)} %pad_clamp_fusion.4), kind=kCustom, calls=%fused_computation.1.clone.1 | custom fusion | bytes 2099200 | tf_op jit(solution)/shard_map/while/body/eval_jaxpr/gather | solution.py:57
  389.5 5.5 %gather_fusion.1 = bf16[512,1024]{1,0:T(8,128)(2,1)S(1)} fusion(bf16[2048,1024]{1,0:T(8,128)(2,1)} %get-tuple-element.218, s32[1024]{0:T(1024)S(1)} %pad_clamp_fusion.5), kind=kCustom, calls=%fused_computation.clone.1 | custom fusion | bytes 2099200 | tf_op jit(solution)/shard_map/while/body/eval_jaxpr/gather | solution.py:56
  396.3 1.2 fusion.56
  397.5 5.5 %gather_fusion = bf16[512,1024]{1,0:T(8,128)(2,1)S(1)} fusion(bf16[2048,1024]{1,0:T(8,128)(2,1)} %get-tuple-element.218, s32[1024]{0:T(1024)S(1)} %pad_clamp_fusion.4), kind=kCustom, calls=%fused_computation.1.clone.1 | custom fusion | bytes 2099200 | tf_op jit(solution)/shard_map/while/body/eval_jaxpr/gather | solution.py:57
  403.2 5.5 %gather_fusion.1 = bf16[512,1024]{1,0:T(8,128)(2,1)S(1)} fusion(bf16[2048,1024]{1,0:T(8,128)(2,1)} %get-tuple-element.218, s32[1024]{0:T(1024)S(1)} %pad_clamp_fusion.5), kind=kCustom, calls=%fused_computation.clone.1 | custom fusion | bytes 2099200 | tf_op jit(solution)/shard_map/while/body/eval_jaxpr/gather | solution.py:56
  410.0 1.2 fusion.56
  (200 shorter events, 22.9 us)
Async XLA Ops:
  6.5 8.6 %copy-start.4 = (bf16[8,3,64]{2,0,1:T(8,128)(2,1)S(1)}, bf16[8,3,64]{2,0,1:T(8,128)(2,1)}, u32[]{:S(2)}) copy-start(bf16[8,3,64]{2,0,1:T(8,128)(2,1)} %param.10) | copy-start | bytes 9220
  6.5 8.6 %copy-start.2 = (bf16[8,1024]{1,0:T(8,128)(2,1)S(1)}, bf16[8,1024]{1,0:T(8,128)(2,1)}, u32[]{:S(2)}) copy-start(bf16[8,1024]{1,0:T(8,128)(2,1)} %param.11) | copy-start | bytes 49156
  6.5 8.7 %copy-start.3 = (s32[32,64]{1,0:T(8,128)S(1)}, s32[32,64]{1,0:T(8,128)}, u32[]{:S(2)}) copy-start(s32[32,64]{1,0:T(8,128)} %param.12) | copy-start | bytes 24580
  30.1 8.2 %copy-start.1 = (s32[2,8192]{1,0:T(2,128)S(1)}, s32[2,8192]{1,0:T(2,128)}, u32[]{:S(2)}) copy-start(s32[2,8192]{1,0:T(2,128)} %param.15) | copy-start | bytes 196612
  30.1 8.4 %copy-start.5 = (s32[64]{0:T(128)S(1)}, s32[64]{0:T(128)}, u32[]{:S(2)}) copy-start(s32[64]{0:T(128)} %param.14) | copy-start | bytes 772
  30.1 159.7 %copy-start.6 = (s32[64]{0:T(128)S(1)}, s32[64]{0:T(128)}, u32[]{:S(2)}) copy-start(s32[64]{0:T(128)} %param.13) | copy-start | bytes 772
  30.1 160.9 %all-to-all-start = ((bf16[32,64,1024]{2,1,0:T(8,128)(2,1)}), bf16[32,64,1024]{2,1,0:T(8,128)(2,1)}, u32[]{:S(2)}, u32[]{:S(2)}) async-start(bf16[32,64,1024]{2,1,0:T(8,128)(2,1)} %bitcast.58), calls=%async_computation | async-start | bytes 8388608 | tf_op jit(solution)/shard_map/all_to_all | solution.py:89
  37.6 152.3 %all-reduce.2.cloned.1.call-start = ((), (), s32[]{:S(2)}) async-start(), calls=%async_computation.1 | async-start | bytes 262144 | tf_op jit(solution)/shard_map/psum | solution.py:84
  202.6 1.0 copy-start
  216.3 1.0 copy-start
  230.1 1.0 copy-start
  243.9 1.0 copy-start
  257.6 1.0 copy-start
  271.4 1.0 copy-start
  285.1 1.0 copy-start
  298.9 1.0 copy-start
  312.7 1.0 copy-start
  326.4 1.0 copy-start
  340.2 1.0 copy-start
  353.9 1.0 copy-start
  367.7 1.0 copy-start
  381.5 1.0 copy-start
  395.2 1.0 copy-start
  409.0 1.0 copy-start
Sparse Core Ops, SparseCore 0:
  43.9 145.8 all-reduce.1
where the time goes:
time: 420 us; the launch traced here: 418 us
  local copies, waits for them, and re-layouts  191 us (45%)
  waiting for transfers between devices  149 us (35%)
  other arithmetic  33.9 us (8%)
  matrix products  22.1 us (5%)
  between operations  13.6 us (3%)
  starting transfers between devices  7.5 us (2%)
    psum x1, waiting for transfers between devices, shards(): power_sum = lax.psum(local_power, 'ev')  148 us
    gather x16, local copies, waits for them, and re-layouts, correlate_group(): second_spec = spectra[second_rows].astype(jnp.float32)  87.3 us
    gather x16, local copies, waits for them, and re-layouts, correlate_group(): first_spec = spectra[first_rows].astype(jnp.float32)  87.3 us
    another operation x18, other arithmetic  19.9 us
    dot_general x16, matrix products, correlate_group(): lagged = jnp.dot(cross_spec, lag_tab, preferred_element_type=jnp.float32)  19.7 us
    gather x1, local copies, waits for them, and re-layouts, shards(): own_rows[send_rows]  9.66 us
  transfers between devices with their start and end apart: 2, of which 1 were waited for; matrix products, arithmetic and copies ran while one was open for 1% of the time, Pallas kernels for 0%

commit v1 on v0

--- a/solution.py
+++ b/solution.py
@@ -1,3 +1,4 @@
+import functools
 from functools import partial
 import math
 import jax
@@ -7,6 +8,13 @@
 
 LAGS = 255
 epsilon = 1e-06
+
+
+def update_quarters(in_array, axis_key):
+    return lax.all_gather(in_array, axis_name=axis_key).sum(axis=0)
+
+
+unite_bars = functools.partial(update_quarters, axis_key="ev")
 
 
 def spectral_table(length):
@@ -81,7 +89,7 @@
     local_power = jnp.sum(
         deconvolved[..., :half_len] ** 2 + deconvolved[..., half_len:] ** 2, axis=0
     )
-    power_sum = lax.psum(local_power, "ev")
+    power_sum = unite_bars(local_power)
     weight = 1.0 / (power_sum / (ev_dev * owners) + epsilon)
     capacity = send_rows.shape[1]
     slot_total = owners * capacity

time: 420 us -> 378 us (0.900)
  waiting for transfers between devices: 149 us -> 105 us
    psum x1 -> x0, waiting for transfers between devices: 148 us -> none  [shards(): power_sum = lax.psum(local_power, 'ev')]
    all_gather x0 -> x1, waiting for transfers between devices: none -> 76.5 us  [update_quarters(): return lax.all_gather(in_array, axis_name=axis_key).sum(axis=0)]
    all_to_all x1, waiting for transfers between devices: 0.01 us -> 28.6 us  [shards(): lax.all_to_all(own_rows[send_rows], 'ev', split_axis=0, concat_axis=0, ti...]
  transfers between devices with their start and end apart: 2 -> 2, of which waited for: 1 -> 2; matrix products, arithmetic and copies ran while one was open for 1% -> 4% of each run, Pallas kernels for 0% -> 0%
where the time goes in v1:
time: 378 us; the launch traced here: 376 us
  local copies, waits for them, and re-layouts  191 us (51%)
  waiting for transfers between devices  105 us (28%)
  other arithmetic  36.5 us (10%)
  matrix products  21.2 us (6%)
  between operations  13.6 us (4%)
  starting transfers between devices  7.46 us (2%)
    gather x16, local copies, waits for them, and re-layouts, correlate_group(): second_spec = spectra[second_rows].astype(jnp.float32)  87.3 us
    gather x16, local copies, waits for them, and re-layouts, correlate_group(): first_spec = spectra[first_rows].astype(jnp.float32)  87.3 us
    all_gather x1, waiting for transfers between devices, update_quarters(): return lax.all_gather(in_array, axis_name=axis_key).sum(axis=0)  76.5 us
    all_to_all x1, waiting for transfers between devices, shards(): lax.all_to_all(own_rows[send_rows], 'ev', split_axis=0, concat_axis=0, ti...  28.6 us
    another operation x18, other arithmetic  19.9 us
    dot_general x16, matrix products, correlate_group(): lagged = jnp.dot(cross_spec, lag_tab, preferred_element_type=jnp.float32)  19.7 us
    gather x1, local copies, waits for them, and re-layouts, shards(): own_rows[send_rows]  9.63 us
  transfers between devices with their start and end apart: 2, of which 2 were waited for; matrix products, arithmetic and copies ran while one was open for 4% of the time, Pallas kernels for 0%

profile of v1, /device:TPU:0, one launch (start us, length us, event | category | flops | bytes accessed | tf_op | source)
XLA Modules:
  0.0 376.1 jit_solution(6486373038938365218)
XLA Ops:
  6.5 8.6 %multiply_convert_fusion = (bf16[1024,512]{1,0:T(8,128)(2,1)S(1)}, bf16[1024,512]{1,0:T(8,128)(2,1)S(1)}) fusion(), kind=kLoop, calls=%fused_computation.38 | loop fusion | flops 9961472 | bytes 2097152 | tf_op jit(solution)/shard_map/convert.10
  15.2 2.7 multiply_reduce_fusion
  17.9 1.2 fusion.16
  19.2 1.1 add_reduce_fusion
  20.5 9.6 %gather_fusion.2 = bf16[2048,1024]{1,0:T(8,128)(2,1)} fusion(bf16[512,1024]{1,0:T(8,128)(2,1)S(1)} %pad_maximum_fusion, s32[2048]{0:T(1024)S(1)} %broadcast_clamp_fusion), kind=kCustom, calls=%fused_computation.2 | custom fusion | bytes 8396800 | tf_op jit(solution)/shard_map/gather | solution.py:97
  30.2 7.5 %all-to-all-start = ((bf16[32,64,1024]{2,1,0:T(8,128)(2,1)}), bf16[32,64,1024]{2,1,0:T(8,128)(2,1)}, u32[]{:S(2)}, u32[]{:S(2)}) async-start(bf16[32,64,1024]{2,1,0:T(8,128)(2,1)} %bitcast.59), calls=%async_computation | async-start | bytes 8388608 | tf_op jit(solution)/shard_map/all_to_all | solution.py:97
  37.9 2.3 multiply_convert_fusion.3
  40.2 0.9 pad_maximum_fusion.1
  41.1 76.5 %all-gather.3.cloned.1.call-done = f32[2048,512]{1,0:T(8,128)} async-done(((f32[64,512]{1,0:T(8,128)}), f32[2048,512]{1,0:T(8,128)}) %all-gather.3.cloned.1.call-update) | async-done | bytes 4194320 | tf_op jit(solution)/shard_map/all_gather | solution.py:14
  117.6 2.5 reduce_sum.29
  120.4 28.6 %all-to-all-done = bf16[32,64,1024]{2,1,0:T(8,128)(2,1)} async-done(((bf16[32,64,1024]{2,1,0:T(8,128)(2,1)}), bf16[32,64,1024]{2,1,0:T(8,128)(2,1)}, u32[]{:S(2)}, u32[]{:S(2)}) %all-to-all-start) | async-done | bytes 4194336 | tf_op jit(solution)/shard_map/all_to_all | solution.py:97
  149.0 220.2 %while.12 = (s32[]{:T(128)}, f32[16,512,255]{2,1,0:T(8,128)}, s32[16,4]{1,0:T(8,128)S(1)}, s32[16,512]{1,0:T(8,128)S(1)}, bf16[2048,1024]{1,0:T(8,128)(2,1)}, /*...) while((s32[]{:T(128)}, f32[16,512,255]{2,1,0:T(8,128)}, ...), condition=%wide.region_4.5_spmd, body=%wide.region_3.4_spmd.sunk | while | flops 273293312 | bytes 19963572 | solution.py:108
  149.1 5.5 %gather_fusion = bf16[512,1024]{1,0:T(8,128)(2,1)S(1)} fusion(bf16[2048,1024]{1,0:T(8,128)(2,1)} %get-tuple-element.218, s32[1024]{0:T(1024)S(1)} %pad_clamp_fusion.4), kind=kCustom, calls=%fused_computation.1.clone.1 | custom fusion | bytes 2099200 | tf_op jit(solution)/shard_map/while/body/eval_jaxpr/gather | solution.py:65
  154.8 5.5 %gather_fusion.1 = bf16[512,1024]{1,0:T(8,128)(2,1)S(1)} fusion(bf16[2048,1024]{1,0:T(8,128)(2,1)} %get-tuple-element.218, s32[1024]{0:T(1024)S(1)} %pad_clamp_fusion.5), kind=kCustom, calls=%fused_computation.clone.1 | custom fusion | bytes 2099200 | tf_op jit(solution)/shard_map/while/body/eval_jaxpr/gather | solution.py:64
  160.5 0.6 fusion.53
  161.6 1.2 fusion.56
  162.8 5.5 %gather_fusion = bf16[512,1024]{1,0:T(8,128)(2,1)S(1)} fusion(bf16[2048,1024]{1,0:T(8,128)(2,1)} %get-tuple-element.218, s32[1024]{0:T(1024)S(1)} %pad_clamp_fusion.4), kind=kCustom, calls=%fused_computation.1.clone.1 | custom fusion | bytes 2099200 | tf_op jit(solution)/shard_map/while/body/eval_jaxpr/gather | solution.py:65
  168.6 5.5 %gather_fusion.1 = bf16[512,1024]{1,0:T(8,128)(2,1)S(1)} fusion(bf16[2048,1024]{1,0:T(8,128)(2,1)} %get-tuple-element.218, s32[1024]{0:T(1024)S(1)} %pad_clamp_fusion.5), kind=kCustom, calls=%fused_computation.clone.1 | custom fusion | bytes 2099200 | tf_op jit(solution)/shard_map/while/body/eval_jaxpr/gather | solution.py:64
  174.3 0.6 fusion.53
  175.3 1.2 fusion.56
  176.6 5.5 %gather_fusion = bf16[512,1024]{1,0:T(8,128)(2,1)S(1)} fusion(bf16[2048,1024]{1,0:T(8,128)(2,1)} %get-tuple-element.218, s32[1024]{0:T(1024)S(1)} %pad_clamp_fusion.4), kind=kCustom, calls=%fused_computation.1.clone.1 | custom fusion | bytes 2099200 | tf_op jit(solution)/shard_map/while/body/eval_jaxpr/gather | solution.py:65
  182.3 5.5 %gather_fusion.1 = bf16[512,1024]{1,0:T(8,128)(2,1)S(1)} fusion(bf16[2048,1024]{1,0:T(8,128)(2,1)} %get-tuple-element.218, s32[1024]{0:T(1024)S(1)} %pad_clamp_fusion.5), kind=kCustom, calls=%fused_computation.clone.1 | custom fusion | bytes 2099200 | tf_op jit(solution)/shard_map/while/body/eval_jaxpr/gather | solution.py:64
  188.1 0.6 fusion.53
  189.1 1.2 fusion.56
  190.4 5.5 %gather_fusion = bf16[512,1024]{1,0:T(8,128)(2,1)S(1)} fusion(bf16[2048,1024]{1,0:T(8,128)(2,1)} %get-tuple-element.218, s32[1024]{0:T(1024)S(1)} %pad_clamp_fusion.4), kind=kCustom, calls=%fused_computation.1.clone.1 | custom fusion | bytes 2099200 | tf_op jit(solution)/shard_map/while/body/eval_jaxpr/gather | solution.py:65
  196.1 5.5 %gather_fusion.1 = bf16[512,1024]{1,0:T(8,128)(2,1)S(1)} fusion(bf16[2048,1024]{1,0:T(8,128)(2,1)} %get-tuple-element.218, s32[1024]{0:T(1024)S(1)} %pad_clamp_fusion.5), kind=kCustom, calls=%fused_computation.clone.1 | custom fusion | bytes 2099200 | tf_op jit(solution)/shard_map/while/body/eval_jaxpr/gather | solution.py:64
  202.9 1.2 fusion.56
  204.1 5.5 %gather_fusion = bf16[512,1024]{1,0:T(8,128)(2,1)S(1)} fusion(bf16[2048,1024]{1,0:T(8,128)(2,1)} %get-tuple-element.218, s32[1024]{0:T(1024)S(1)} %pad_clamp_fusion.4), kind=kCustom, calls=%fused_computation.1.clone.1 | custom fusion | bytes 2099200 | tf_op jit(solution)/shard_map/while/body/eval_jaxpr/gather | solution.py:65
  209.8 5.5 %gather_fusion.1 = bf16[512,1024]{1,0:T(8,128)(2,1)S(1)} fusion(bf16[2048,1024]{1,0:T(8,128)(2,1)} %get-tuple-element.218, s32[1024]{0:T(1024)S(1)} %pad_clamp_fusion.5), kind=kCustom, calls=%fused_computation.clone.1 | custom fusion | bytes 2099200 | tf_op jit(solution)/shard_map/while/body/eval_jaxpr/gather | solution.py:64
  215.6 0.6 fusion.53
  216.6 1.2 fusion.56
  217.9 5.5 %gather_fusion = bf16[512,1024]{1,0:T(8,128)(2,1)S(1)} fusion(bf16[2048,1024]{1,0:T(8,128)(2,1)} %get-tuple-element.218, s32[1024]{0:T(1024)S(1)} %pad_clamp_fusion.4), kind=kCustom, calls=%fused_computation.1.clone.1 | custom fusion | bytes 2099200 | tf_op jit(solution)/shard_map/while/body/eval_jaxpr/gather | solution.py:65
  223.6 5.5 %gather_fusion.1 = bf16[512,1024]{1,0:T(8,128)(2,1)S(1)} fusion(bf16[2048,1024]{1,0:T(8,128)(2,1)} %get-tuple-element.218, s32[1024]{0:T(1024)S(1)} %pad_clamp_fusion.5), kind=kCustom, calls=%fused_computation.clone.1 | custom fusion | bytes 2099200 | tf_op jit(solution)/shard_map/while/body/eval_jaxpr/gather | solution.py:64
  230.4 1.2 fusion.56
  231.6 5.5 %gather_fusion = bf16[512,1024]{1,0:T(8,128)(2,1)S(1)} fusion(bf16[2048,1024]{1,0:T(8,128)(2,1)} %get-tuple-element.218, s32[1024]{0:T(1024)S(1)} %pad_clamp_fusion.4), kind=kCustom, calls=%fused_computation.1.clone.1 | custom fusion | bytes 2099200 | tf_op jit(solution)/shard_map/while/body/eval_jaxpr/gather | solution.py:65
  237.4 5.5 %gather_fusion.1 = bf16[512,1024]{1,0:T(8,128)(2,1)S(1)} fusion(bf16[2048,1024]{1,0:T(8,128)(2,1)} %get-tuple-element.218, s32[1024]{0:T(1024)S(1)} %pad_clamp_fusion.5), kind=kCustom, calls=%fused_computation.clone.1 | custom fusion | bytes 2099200 | tf_op jit(solution)/shard_map/while/body/eval_jaxpr/gather | solution.py:64
  244.1 1.2 fusion.56
  245.4 5.5 %gather_fusion = bf16[512,1024]{1,0:T(8,128)(2,1)S(1)} fusion(bf16[2048,1024]{1,0:T(8,128)(2,1)} %get-tuple-element.218, s32[1024]{0:T(1024)S(1)} %pad_clamp_fusion.4), kind=kCustom, calls=%fused_computation.1.clone.1 | custom fusion | bytes 2099200 | tf_op jit(solution)/shard_map/while/body/eval_jaxpr/gather | solution.py:65
  251.1 5.5 %gather_fusion.1 = bf16[512,1024]{1,0:T(8,128)(2,1)S(1)} fusion(bf16[2048,1024]{1,0:T(8,128)(2,1)} %get-tuple-element.218, s32[1024]{0:T(1024)S(1)} %pad_clamp_fusion.5), kind=kCustom, calls=%fused_computation.clone.1 | custom fusion | bytes 2099200 | tf_op jit(solution)/shard_map/while/body/eval_jaxpr/gather | solution.py:64
  257.9 1.2 fusion.56
  259.2 5.5 %gather_fusion = bf16[512,1024]{1,0:T(8,128)(2,1)S(1)} fusion(bf16[2048,1024]{1,0:T(8,128)(2,1)} %get-tuple-element.218, s32[1024]{0:T(1024)S(1)} %pad_clamp_fusion.4), kind=kCustom, calls=%fused_computation.1.clone.1 | custom fusion | bytes 2099200 | tf_op jit(solution)/shard_map/while/body/eval_jaxpr/gather | solution.py:65
  264.9 5.5 %gather_fusion.1 = bf16[512,1024]{1,0:T(8,128)(2,1)S(1)} fusion(bf16[2048,1024]{1,0:T(8,128)(2,1)} %get-tuple-element.218, s32[1024]{0:T(1024)S(1)} %pad_clamp_fusion.5), kind=kCustom, calls=%fused_computation.clone.1 | custom fusion | bytes 2099200 | tf_op jit(solution)/shard_map/while/body/eval_jaxpr/gather | solution.py:64
  271.7 1.2 fusion.56
  272.9 5.5 %gather_fusion = bf16[512,1024]{1,0:T(8,128)(2,1)S(1)} fusion(bf16[2048,1024]{1,0:T(8,128)(2,1)} %get-tuple-element.218, s32[1024]{0:T(1024)S(1)} %pad_clamp_fusion.4), kind=kCustom, calls=%fused_computation.1.clone.1 | custom fusion | bytes 2099200 | tf_op jit(solution)/shard_map/while/body/eval_jaxpr/gather | solution.py:65
  278.6 5.5 %gather_fusion.1 = bf16[512,1024]{1,0:T(8,128)(2,1)S(1)} fusion(bf16[2048,1024]{1,0:T(8,128)(2,1)} %get-tuple-element.218, s32[1024]{0:T(1024)S(1)} %pad_clamp_fusion.5), kind=kCustom, calls=%fused_computation.clone.1 | custom fusion | bytes 2099200 | tf_op jit(solution)/shard_map/while/body/eval_jaxpr/gather | solution.py:64
  285.4 1.2 fusion.56
  286.7 5.5 %gather_fusion = bf16[512,1024]{1,0:T(8,128)(2,1)S(1)} fusion(bf16[2048,1024]{1,0:T(8,128)(2,1)} %get-tuple-element.218, s32[1024]{0:T(1024)S(1)} %pad_clamp_fusion.4), kind=kCustom, calls=%fused_computation.1.clone.1 | custom fusion | bytes 2099200 | tf_op jit(solution)/shard_map/while/body/eval_jaxpr/gather | solution.py:65
  292.4 5.5 %gather_fusion.1 = bf16[512,1024]{1,0:T(8,128)(2,1)S(1)} fusion(bf16[2048,1024]{1,0:T(8,128)(2,1)} %get-tuple-element.218, s32[1024]{0:T(1024)S(1)} %pad_clamp_fusion.5), kind=kCustom, calls=%fused_computation.clone.1 | custom fusion | bytes 2099200 | tf_op jit(solution)/shard_map/while/body/eval_jaxpr/gather | solution.py:64
  299.2 1.2 fusion.56
  300.4 5.5 %gather_fusion = bf16[512,1024]{1,0:T(8,128)(2,1)S(1)} fusion(bf16[2048,1024]{1,0:T(8,128)(2,1)} %get-tuple-element.218, s32[1024]{0:T(1024)S(1)} %pad_clamp_fusion.4), kind=kCustom, calls=%fused_computation.1.clone.1 | custom fusion | bytes 2099200 | tf_op jit(solution)/shard_map/while/body/eval_jaxpr/gather | solution.py:65
  306.2 5.5 %gather_fusion.1 = bf16[512,1024]{1,0:T(8,128)(2,1)S(1)} fusion(bf16[2048,1024]{1,0:T(8,128)(2,1)} %get-tuple-element.218, s32[1024]{0:T(1024)S(1)} %pad_clamp_fusion.5), kind=kCustom, calls=%fused_computation.clone.1 | custom fusion | bytes 2099200 | tf_op jit(solution)/shard_map/while/body/eval_jaxpr/gather | solution.py:64
  312.9 1.2 fusion.56
  314.2 5.5 %gather_fusion = bf16[512,1024]{1,0:T(8,128)(2,1)S(1)} fusion(bf16[2048,1024]{1,0:T(8,128)(2,1)} %get-tuple-element.218, s32[1024]{0:T(1024)S(1)} %pad_clamp_fusion.4), kind=kCustom, calls=%fused_computation.1.clone.1 | custom fusion | bytes 2099200 | tf_op jit(solution)/shard_map/while/body/eval_jaxpr/gather | solution.py:65
  319.9 5.5 %gather_fusion.1 = bf16[512,1024]{1,0:T(8,128)(2,1)S(1)} fusion(bf16[2048,1024]{1,0:T(8,128)(2,1)} %get-tuple-element.218, s32[1024]{0:T(1024)S(1)} %pad_clamp_fusion.5), kind=kCustom, calls=%fused_computation.clone.1 | custom fusion | bytes 2099200 | tf_op jit(solution)/shard_map/while/body/eval_jaxpr/gather | solution.py:64
  326.7 1.2 fusion.56
  328.0 5.5 %gather_fusion = bf16[512,1024]{1,0:T(8,128)(2,1)S(1)} fusion(bf16[2048,1024]{1,0:T(8,128)(2,1)} %get-tuple-element.218, s32[1024]{0:T(1024)S(1)} %pad_clamp_fusion.4), kind=kCustom, calls=%fused_computation.1.clone.1 | custom fusion | bytes 2099200 | tf_op jit(solution)/shard_map/while/body/eval_jaxpr/gather | solution.py:65
  333.7 5.5 %gather_fusion.1 = bf16[512,1024]{1,0:T(8,128)(2,1)S(1)} fusion(bf16[2048,1024]{1,0:T(8,128)(2,1)} %get-tuple-element.218, s32[1024]{0:T(1024)S(1)} %pad_clamp_fusion.5), kind=kCustom, calls=%fused_computation.clone.1 | custom fusion | bytes 2099200 | tf_op jit(solution)/shard_map/while/body/eval_jaxpr/gather | solution.py:64
  340.5 1.2 fusion.56
  341.7 5.5 %gather_fusion = bf16[512,1024]{1,0:T(8,128)(2,1)S(1)} fusion(bf16[2048,1024]{1,0:T(8,128)(2,1)} %get-tuple-element.218, s32[1024]{0:T(1024)S(1)} %pad_clamp_fusion.4), kind=kCustom, calls=%fused_computation.1.clone.1 | custom fusion | bytes 2099200 | tf_op jit(solution)/shard_map/while/body/eval_jaxpr/gather | solution.py:65
  347.4 5.5 %gather_fusion.1 = bf16[512,1024]{1,0:T(8,128)(2,1)S(1)} fusion(bf16[2048,1024]{1,0:T(8,128)(2,1)} %get-tuple-element.218, s32[1024]{0:T(1024)S(1)} %pad_clamp_fusion.5), kind=kCustom, calls=%fused_computation.clone.1 | custom fusion | bytes 2099200 | tf_op jit(solution)/shard_map/while/body/eval_jaxpr/gather | solution.py:64
  354.2 1.2 fusion.56
  355.5 5.5 %gather_fusion = bf16[512,1024]{1,0:T(8,128)(2,1)S(1)} fusion(bf16[2048,1024]{1,0:T(8,128)(2,1)} %get-tuple-element.218, s32[1024]{0:T(1024)S(1)} %pad_clamp_fusion.4), kind=kCustom, calls=%fused_computation.1.clone.1 | custom fusion | bytes 2099200 | tf_op jit(solution)/shard_map/while/body/eval_jaxpr/gather | solution.py:65
  361.2 5.5 %gather_fusion.1 = bf16[512,1024]{1,0:T(8,128)(2,1)S(1)} fusion(bf16[2048,1024]{1,0:T(8,128)(2,1)} %get-tuple-element.218, s32[1024]{0:T(1024)S(1)} %pad_clamp_fusion.5), kind=kCustom, calls=%fused_computation.clone.1 | custom fusion | bytes 2099200 | tf_op jit(solution)/shard_map/while/body/eval_jaxpr/gather | solution.py:64
  368.0 1.2 fusion.56
  (201 shorter events, 23.2 us)
Async XLA Ops:
  6.5 8.6 %copy-start.4 = (bf16[8,3,64]{2,0,1:T(8,128)(2,1)S(1)}, bf16[8,3,64]{2,0,1:T(8,128)(2,1)}, u32[]{:S(2)}) copy-start(bf16[8,3,64]{2,0,1:T(8,128)(2,1)} %param.10) | copy-start | bytes 9220
  6.5 8.6 %copy-start.2 = (bf16[8,1024]{1,0:T(8,128)(2,1)S(1)}, bf16[8,1024]{1,0:T(8,128)(2,1)}, u32[]{:S(2)}) copy-start(bf16[8,1024]{1,0:T(8,128)(2,1)} %param.11) | copy-start | bytes 49156
  6.5 111.0 %all-gather.3.cloned.1.call-start = ((), (), s32[]{:S(2)}) async-start(), calls=%async_computation.1 | async-start | bytes 4325376 | tf_op jit(solution)/shard_map/all_gather | solution.py:14
  19.2 1.1 copy-start.3
  30.2 7.5 %copy-start.1 = (s32[2,8192]{1,0:T(2,128)S(1)}, s32[2,8192]{1,0:T(2,128)}, u32[]{:S(2)}) copy-start(s32[2,8192]{1,0:T(2,128)} %param.15) | copy-start | bytes 196612
  30.2 7.7 %copy-start.5 = (s32[64]{0:T(128)S(1)}, s32[64]{0:T(128)}, u32[]{:S(2)}) copy-start(s32[64]{0:T(128)} %param.14) | copy-start | bytes 772
  30.2 118.9 %all-to-all-start = ((bf16[32,64,1024]{2,1,0:T(8,128)(2,1)}), bf16[32,64,1024]{2,1,0:T(8,128)(2,1)}, u32[]{:S(2)}, u32[]{:S(2)}) async-start(bf16[32,64,1024]{2,1,0:T(8,128)(2,1)} %bitcast.59), calls=%async_computation | async-start | bytes 8388608 | tf_op jit(solution)/shard_map/all_to_all | solution.py:97
  117.6 2.5 copy-start.6
  160.5 1.0 copy-start
  174.3 1.0 copy-start
  188.1 1.0 copy-start
  201.8 1.0 copy-start
  215.6 1.0 copy-start
  229.3 1.0 copy-start
  243.1 1.0 copy-start
  256.9 1.0 copy-start
  270.6 1.0 copy-start
  284.4 1.0 copy-start
  298.1 1.0 copy-start
  311.9 1.0 copy-start
  325.7 1.0 copy-start
  339.4 1.0 copy-start
  353.2 1.0 copy-start
  366.9 1.0 copy-start
Sparse Core Ops, SparseCore 0:
  20.4 97.1 all-gather.2
